TPU v7x, 32 devices: a whole 2x2x4 slice. The times are simulated.
32 devices in a mesh: ctx: 8 (over y, x, core), grp: 4 (over z).
Axes of the slice: x: 2, y: 2, z: 4, core: 2. Of those that a mesh axis runs over, the one named last changes fastest.
Arguments:
- window_states: bfloat16 [4, 64, 8192], P('grp'), may hold values from -6 to 6
- query_weight: bfloat16 [8192, 8192], P('grp', 'ctx'), may hold values from -0.0625 to 0.0625
- cache_keys: bfloat16 [4, 4096, 1024], P('grp', 'ctx'), may hold values from -65 to 65
- cache_values: bfloat16 [4, 4096, 1024], P('grp', 'ctx'), may hold values from -6 to 6
- kept_blocks: int32 [4, 8, 8], P('grp', None, 'ctx'), may hold values from 0 to 31, as said below
- retained_block_count: int32 [4, 8, 8], P('grp', None, 'ctx'), may hold values from 0 to 1, as said below
- decode_queries: bfloat16 [4, 4, 8, 8192], P('grp', None, 'ctx'), may hold values from -9 to 9
- tail_keys: bfloat16 [4, 8, 64, 1024], P('grp', 'ctx'), may hold values from -6 to 6
- tail_values: bfloat16 [4, 8, 64, 1024], P('grp', 'ctx'), may hold values from -6 to 6
- row_lengths: int32 [4, 8], P('grp', 'ctx'), may hold values from 2 to 61, as said below
Outputs:
- pooled_votes: float32 [4, 8, 4096], P('grp', None, 'ctx')
- decode_out: bfloat16 [4, 4, 8, 8192], P('grp', None, 'ctx')
Inputs may be any that keep to these rules, and one draw needn't show every extreme that they name: `kept_blocks`: for key head k, entry c names one block held by ctx index c, that is one of the blocks c * 4 to c * 4 + 3; it is kept only if retained_block_count[g, k, c] is 1. `retained_block_count`: in every request some device holds 1 kept blocks for every key head. `row_lengths`: 61 is reached in every request.
All inputs are finite; a program needn't handle non-finite values.
Results may differ from a plain program's by a relative error of at most 0.0019.
Values may be sent and summed in bfloat16 or wider, within the bound.
No kernel may reach another device: no remote copies, remote signals or barrier semaphores. Data moves between devices by JAX's collectives and lax.ppermute only.
A program may use at most 128 MiB of HBM per device.

v0:
```python
import math

import jax
import jax.numpy as jnp
from jax import lax
from jax.sharding import PartitionSpec as P

KEY_HEADS = 8
HEAD_DIMENSION = 128
BLOCK_POSITIONS = 128
POOL = 7


def combined_all(part, axis, combine):
    gathered = jax.tree.map(lambda a: lax.all_gather(a, axis), part)

    def take(source):
        return jax.tree.map(lambda a: lax.dynamic_index_in_dim(a, source, 0, False), gathered)

    return lax.fori_loop(
        1, lax.axis_size(axis), lambda source, state: combine(state, take(source)), take(0)
    )


def padded_2(cells, sides, width):
    for axis, dim in sides:
        count = lax.axis_size(axis)
        ends = count - 1
        head = lax.slice_in_dim(cells, 0, width, axis=dim)
        tail = lax.slice_in_dim(cells, cells.shape[dim] - width, cells.shape[dim], axis=dim)
        cells = jnp.concatenate(
            [
                lax.ppermute(tail, axis, [(i, (i + 1) % count) for i in range(ends)]),
                cells,
                lax.ppermute(head, axis, [((i + 1) % count, i) for i in range(ends)]),
            ],
            axis=dim,
        )
    return cells


def rotary_table(positions, head_size):
    exponent = jnp.arange(0, head_size, 2).astype(jnp.float32) / head_size
    inverse = jnp.power(jnp.float32(500000.0), -exponent)
    wavelength = 2.0 * math.pi / inverse
    smooth = (8192.0 / wavelength - 1.0) / 3.0
    blended = (1.0 - smooth) * inverse / 8.0 + smooth * inverse
    adjusted = jnp.where(
        wavelength > 8192.0, inverse / 8.0, jnp.where(wavelength < 2048.0, inverse, blended)
    )
    angles = positions[:, None] * adjusted[None, :]
    return (jnp.cos(angles), jnp.sin(angles))


def rotate(vectors, cosine_table, sine_table):
    half_size = vectors.shape[-1] // 2
    leading = vectors[..., :half_size]
    trailing = vectors[..., half_size:]
    cosine_part = cosine_table[:, None, :]
    sine_part = sine_table[:, None, :]
    return jnp.concatenate(
        [
            leading * cosine_part - trailing * sine_part,
            trailing * cosine_part + leading * sine_part,
        ],
        axis=-1,
    )


def merge_stats(earlier, later):
    highest = jnp.maximum(earlier[0], later[0])
    return (
        highest,
        earlier[1] * jnp.exp(earlier[0] - highest) + later[1] * jnp.exp(later[0] - highest),
    )


def on_device(
    window_states,
    query_weight,
    cache_keys,
    cache_values,
    kept_blocks,
    retained_block_count,
    decode_queries,
    tail_keys,
    tail_values,
    row_lengths,
):
    ctx_count = lax.axis_size("ctx")
    ctx_index = lax.axis_index("ctx")
    states = window_states[0]
    win_rows = states.shape[0]
    local_cols = query_weight.shape[1]
    local_heads = local_cols // HEAD_DIMENSION
    projected = jnp.dot(
        states,
        lax.all_gather(query_weight, "grp", axis=0, tiled=True),
        preferred_element_type=jnp.float32,
    )
    local_keys = cache_keys[0]
    ctx_local = local_keys.shape[0]
    total_ctx = ctx_local * ctx_count
    start_pos = total_ctx - win_rows
    positions = (jnp.arange(win_rows) + start_pos).astype(jnp.float32)
    cosine_table, sine_table = rotary_table(positions, HEAD_DIMENSION)
    turned = rotate(
        projected.reshape(win_rows, local_heads, HEAD_DIMENSION), cosine_table, sine_table
    )
    window_local = turned.reshape(win_rows, local_cols).astype(jnp.bfloat16)
    window_all, decode_all = (
        lax.all_gather(window_local, "ctx", axis=1, tiled=True),
        lax.all_gather(decode_queries[0], "ctx", axis=1, tiled=True),
    )
    head_total = window_all.shape[1] // HEAD_DIMENSION
    group_size = head_total // KEY_HEADS
    key_scale = 1.0 / math.sqrt(HEAD_DIMENSION)
    key_positions = ctx_index * ctx_local + jnp.arange(ctx_local)
    allowed = key_positions[None, :] <= (start_pos + jnp.arange(win_rows))[:, None]
    exp_list = []
    max_list = []
    sum_list = []
    for head_index in range(KEY_HEADS):
        head_queries = window_all[
            :,
            head_index
            * group_size
            * HEAD_DIMENSION : (head_index + 1)
            * group_size
            * HEAD_DIMENSION,
        ].reshape(win_rows, group_size, HEAD_DIMENSION)
        key_head_rows = local_keys[
            :, head_index * HEAD_DIMENSION : (head_index + 1) * HEAD_DIMENSION
        ]
        scores = (
            jnp.einsum(
                "wgd,td->gwt", head_queries, key_head_rows, preferred_element_type=jnp.float32
            )
            * key_scale
        )
        scores = jnp.where(allowed[None], scores, -1e30)
        head_max = jnp.max(scores, axis=-1)
        exponent_values = jnp.where(allowed[None], jnp.exp(scores - head_max[..., None]), 0.0)
        exp_list.append(exponent_values)
        max_list.append(head_max)
        sum_list.append(jnp.sum(exponent_values, axis=-1))
    exponentials = jnp.stack(exp_list)
    local_max = jnp.stack(max_list).reshape(head_total, win_rows)
    local_sum = jnp.stack(sum_list).reshape(head_total, win_rows)
    merged_max, merged_sum = combined_all((local_max, local_sum), "ctx", merge_stats)
    coefficient = (jnp.exp(local_max - merged_max) / merged_sum).reshape(
        KEY_HEADS, group_size, win_rows
    )
    vote_sums = jnp.sum(coefficient[..., None] * exponentials, axis=(1, 2)) * (
        total_ctx / (win_rows * group_size)
    )
    half_width = (POOL - 1) // 2
    padded = padded_2(vote_sums, (("ctx", 1),), half_width)
    pooled = padded[:, 0:ctx_local]
    for shift_index in range(1, POOL):
        pooled = pooled + padded[:, shift_index : shift_index + ctx_local]
    pooled_votes = (pooled / POOL)[None]
    step_count = decode_all.shape[0]
    rows_all = decode_all.shape[1]
    rows_local = decode_queries.shape[2]
    total_rows = step_count * rows_all
    block_total = ctx_local // BLOCK_POSITIONS
    keys_local = local_keys.reshape(block_total, BLOCK_POSITIONS, KEY_HEADS, HEAD_DIMENSION)
    values_local = cache_values[0].reshape(block_total, BLOCK_POSITIONS, KEY_HEADS, HEAD_DIMENSION)
    local_blocks = kept_blocks[0] - ctx_index * block_total
    local_counts = retained_block_count[0, :, 0]
    rounds = jnp.max(local_counts)
    grouped = decode_all.reshape(total_rows, KEY_HEADS, group_size, HEAD_DIMENSION)
    head_range = jnp.arange(KEY_HEADS)

    def visit_slot(position, state_now):
        run_max, run_sum, run_acc = state_now
        chosen = lax.dynamic_index_in_dim(local_blocks, position, 1, keepdims=False)
        key_block = keys_local[chosen, :, head_range, :]
        value_block = values_local[chosen, :, head_range, :]
        is_live = (position < local_counts)[None, :, None, None]
        scores = (
            jnp.einsum("rhgd,htd->rhgt", grouped, key_block, preferred_element_type=jnp.float32)
            * key_scale
        )
        scores = jnp.where(is_live, scores, -1e30)
        new_max = jnp.maximum(run_max, jnp.max(scores, axis=-1))
        rescale = jnp.exp(run_max - new_max)
        weights = jnp.where(is_live, jnp.exp(scores - new_max[..., None]), 0.0)
        run_sum = run_sum * rescale + jnp.sum(weights, axis=-1)
        run_acc = run_acc * rescale[..., None] + jnp.einsum(
            "rhgt,htd->rhgd",
            weights,
            value_block.astype(jnp.float32),
            precision=lax.Precision.HIGHEST,
        )
        return (new_max, run_sum, run_acc)

    initial = (
        jnp.full((total_rows, KEY_HEADS, group_size), -1e30, jnp.float32),
        jnp.zeros((total_rows, KEY_HEADS, group_size), jnp.float32),
        jnp.zeros((total_rows, KEY_HEADS, group_size, HEAD_DIMENSION), jnp.float32),
    )
    run_max, run_sum, run_acc = lax.fori_loop(0, rounds, visit_slot, initial)
    cache_max = run_max.reshape(step_count, rows_all, head_total)
    cache_sum = run_sum.reshape(step_count, rows_all, head_total)
    cache_acc = run_acc.reshape(step_count, rows_all, head_total * HEAD_DIMENSION)
    tail_len = tail_keys.shape[2]
    own_queries = decode_queries[0].reshape(
        step_count, rows_local, KEY_HEADS, group_size, HEAD_DIMENSION
    )
    tail_key_rows = tail_keys[0].reshape(rows_local, tail_len, KEY_HEADS, HEAD_DIMENSION)
    tail_value_rows = tail_values[0].reshape(rows_local, tail_len, KEY_HEADS, HEAD_DIMENSION)
    visible = (
        jnp.arange(tail_len)[None, None, :]
        < row_lengths[0][None, :, None] + jnp.arange(step_count)[:, None, None]
    )
    visible = visible[:, :, None, None, :]
    tail_scores = (
        jnp.einsum(
            "srhgd,rjhd->srhgj", own_queries, tail_key_rows, preferred_element_type=jnp.float32
        )
        * key_scale
    )
    tail_scores = jnp.where(visible, tail_scores, -1e30)
    tail_max = jnp.max(tail_scores, axis=-1)
    tail_weights = jnp.where(visible, jnp.exp(tail_scores - tail_max[..., None]), 0.0)
    tail_sum = jnp.sum(tail_weights, axis=-1).reshape(step_count, rows_local, head_total)
    tail_acc = jnp.einsum(
        "srhgj,rjhd->srhgd",
        tail_weights,
        tail_value_rows.astype(jnp.float32),
        precision=lax.Precision.HIGHEST,
    )
    tail_acc = tail_acc.reshape(step_count, rows_local, head_total, HEAD_DIMENSION)
    tail_max = tail_max.reshape(step_count, rows_local, head_total)
    received_acc, received_max, received_sum = (
        lax.all_to_all(cache_acc[None], "ctx", split_axis=2, concat_axis=0, tiled=True),
        lax.all_to_all(cache_max[None], "ctx", split_axis=2, concat_axis=0, tiled=True),
        lax.all_to_all(cache_sum[None], "ctx", split_axis=2, concat_axis=0, tiled=True),
    )
    peak_value = jnp.maximum(jnp.max(received_max, axis=0), tail_max)
    factors = jnp.exp(received_max - peak_value[None])
    tail_factor = jnp.exp(tail_max - peak_value)
    spread_acc = received_acc.reshape(
        received_acc.shape[0], step_count, rows_local, head_total, HEAD_DIMENSION
    )
    numerator = jnp.sum(spread_acc * factors[..., None], axis=0) + tail_acc * tail_factor[..., None]
    denominator = jnp.sum(received_sum * factors, axis=0) + tail_sum * tail_factor
    decode_out = (
        (numerator / denominator[..., None])
        .reshape(step_count, rows_local, head_total * HEAD_DIMENSION)
        .astype(jnp.bfloat16)[None]
    )
    return (pooled_votes, decode_out)


def solution(mesh):
    placed = (
        P("grp", None, None),
        P("grp", "ctx"),
        P("grp", "ctx", None),
        P("grp", "ctx", None),
        P("grp", None, "ctx"),
        P("grp", None, "ctx"),
        P("grp", None, "ctx", None),
        P("grp", "ctx", None, None),
        P("grp", "ctx", None, None),
        P("grp", "ctx"),
    )
    return jax.shard_map(
        on_device,
        mesh=mesh,
        in_specs=placed,
        out_specs=(P("grp", None, "ctx"), P("grp", None, "ctx", None)),
        check_vma=False,
    )
```

profile of v0, /device:TPU:0, one launch (start us, length us, event | category | flops | bytes accessed | tf_op | source)
XLA Modules:
  0.0 408.0 jit_solution(18144013181571954903)
XLA Ops:
  7.9 11.6 %all-gather = bf16[1,4,8,8192]{3,1,0,2:T(4,128)(2,1)S(1)} all-gather(bf16[1,4,1,8192]{3,1,0,2:T(4,128)(2,1)} %bitcast.356), channel_id=2, replica_groups=mesh['ctx'=8,'grp'=4] {'ctx'}, dimensions={2}, use_global_device_ids=true | all-gather | bytes 589824 | tf_op jit(solution)/shard_map/all_gather | solution.py:113
  20.0 1.7 copy.176
  21.9 1.7 copy.178
  24.8 1.3 gather_fusion
  26.1 2.5 gather_fusion.1
  30.7 4.7 %while.34 = (s32[]{:T(128)}, f32[32,8,8]{2,0,1:T(8,128)S(1)}, f32[32,8,8]{2,0,1:T(8,128)S(1)}, f32[32,8,8,128]{3,2,0,1:T(8,128)S(1)}, s32[]{:T(128)}, /*index=5*...) while((s32[]{:T(128)}, f32[32,8,8]{2,0,1:T(8,128)S(1)}, ...), condition=%wide.region_23.24_spmd, body=%wide.region_20.23_spmd.sunk | while | flops 406327296 | bytes 5636265 | solution.py:204
  32.7 2.1 fusion.111
  36.4 3.3 all-to-all-start.1
  44.3 3.9 all-to-all-start.2
  49.0 1.7 copy.144
  53.0 3.6 all-to-all-start
  57.5 1.3 mul.307
  58.8 1.6 mul.308
  60.5 238.6 %all-gather.4.cloned.1.call-done = bf16[8192,1024]{1,0:T(8,128)(2,1)} async-done(((bf16[2048,1024]{1,0:T(8,128)(2,1)}), bf16[8192,1024]{1,0:T(8,128)(2,1)}) %all-gather.4.cloned.1.call-update) | async-done | bytes 16777232 | tf_op jit(solution)/shard_map/all_gather | solution.py:98
  299.1 20.7 %copy.118 = bf16[1024,8192]{1,0:T(8,128)(2,1)} copy(bf16[1024,8192]{0,1:T(8,128)(2,1)} %bitcast.309) | data formatting | bytes 33554432 | tf_op jit(solution)/shard_map/dot_general | solution.py:96
  319.8 8.7 %fusion.36 = f32[64,8,128]{2,0,1:T(8,128)S(1)} fusion(bf16[8,128,8192]{2,1,0:T(8,128)(2,1)} %bitcast.308, bf16[1,64,8192]{2,1,0:T(8,128)(2,1)S(1)} %copy-done), kind=kOutput, calls=%fused_computation.67 | convolution fusion | flops 1073741824 | bytes 18087936 | tf_op jit(solution)/shard_map/dot_general | solution.py:96
  331.0 20.2 %all-gather.6.cloned.1.call-done = bf16[64,8192]{1,0:T(8,128)(2,1)} async-done(((bf16[64,1024]{1,0:T(8,128)(2,1)}), bf16[64,8192]{1,0:T(8,128)(2,1)}) %all-gather.6.cloned.1.call-update) | async-done | bytes 1048592 | tf_op jit(solution)/shard_map/all_gather | solution.py:112
  351.2 1.4 slice_bitcast_fusion.2
  352.6 1.3 fusion.84
  354.0 1.3 fusion.85
  355.3 1.3 fusion.86
  356.7 1.3 fusion.87
  358.1 1.3 fusion.88
  359.5 1.3 fusion.89
  360.8 1.3 fusion.90
  362.2 1.3 fusion.91
  365.6 2.9 fusion.45
  368.8 3.2 copy-done.1
  372.6 9.3 %all_gather.17 = f32[8,64,64]{2,1,0:T(8,128)S(1)} all-gather(f32[1,64,64]{2,1,0:T(8,128)S(1)} %bitcast.343), channel_id=1, replica_groups=mesh['ctx'=8,'grp'=4] {'ctx'}, dimensions={0}, use_global_device_ids=true | all-gather | bytes 147456 | tf_op jit(solution)/shard_map/all_gather | solution.py:15
  382.5 8.4 %all_gather.18 = f32[8,64,64]{2,1,0:T(8,128)S(1)} all-gather(f32[1,64,64]{2,1,0:T(8,128)S(1)} %bitcast.360), channel_id=1, replica_groups=mesh['ctx'=8,'grp'=4] {'ctx'}, dimensions={0}, use_global_device_ids=true | all-gather | bytes 147456 | tf_op jit(solution)/shard_map/all_gather | solution.py:15
  391.4 3.8 multiply_reduce_fusion
  396.6 3.0 collective-permute-start
  (143 shorter events, 24.0 us)
Async XLA Ops:
  7.2 312.7 %copy-start = (bf16[1,64,8192]{2,1,0:T(8,128)(2,1)S(1)}, bf16[1,64,8192]{2,1,0:T(8,128)(2,1)}, u32[]{:S(2)}) copy-start(bf16[1,64,8192]{2,1,0:T(8,128)(2,1)} %param.14) | copy-start | bytes 3145732
  7.2 17.6 %copy-start.3 = (s32[1,8,1]{1,2,0:T(1,128)S(1)}, s32[1,8,1]{1,2,0:T(1,128)}, u32[]{:S(2)}) copy-start(s32[1,8,1]{1,2,0:T(1,128)} %param.18) | copy-start | bytes 100
  7.2 21.5 %copy-start.4 = (s32[1,8,1]{1,2,0:T(1,128)S(1)}, s32[1,8,1]{1,2,0:T(1,128)}, u32[]{:S(2)}) copy-start(s32[1,8,1]{1,2,0:T(1,128)} %param.19) | copy-start | bytes 100
  7.2 291.9 %all-gather.4.cloned.1.call-start = ((), (), s32[]{:S(2)}) async-start(), calls=%async_computation.3 | async-start | bytes 20971520 | tf_op jit(solution)/shard_map/all_gather | solution.py:98
  30.7 11.9 %copy-start.2 = (bf16[1,4,1,8192]{3,1,2,0:T(4,128)(2,1)S(1)}, bf16[1,4,1,8192]{3,1,2,0:T(4,128)(2,1)}, u32[]{:S(2)}) copy-start(bf16[1,4,1,8192]{3,1,2,0:T(4,128)(2,1)} %param.20) | copy-start | bytes 196612
  36.4 8.0 %all-to-all-start.1 = ((f32[8,1,256]{2,1,0:T(1,128)}), f32[8,1,256]{2,1,0:T(1,128)S(1)}, u32[]{:S(2)}, u32[]{:S(2)}) async-start(f32[8,1,256]{2,1,0:T(1,128)} %reshape.469), calls=%async_computation.1 | async-start | bytes 16384 | tf_op jit(solution)/shard_map/all_to_all | solution.py:239
  44.3 8.6 %all-to-all-start.2 = ((f32[8,1,256]{2,1,0:T(1,128)}), f32[8,1,256]{2,1,0:T(1,128)S(1)}, u32[]{:S(2)}, u32[]{:S(2)}) async-start(f32[8,1,256]{2,1,0:T(1,128)} %reshape.471), calls=%async_computation.2 | async-start | bytes 16384 | tf_op jit(solution)/shard_map/all_to_all | solution.py:240
  53.0 276.5 %all-to-all-start = ((f32[1,4,8,8192]{3,1,0,2:T(4,128)}), f32[1,4,8,8192]{3,1,0,2:T(4,128)S(1)}, u32[]{:S(2)}, u32[]{:S(2)}) async-start(f32[1,4,8,8192]{3,1,0,2:T(4,128)} %copy.144), calls=%async_computation | async-start | bytes 2097152 | tf_op jit(solution)/shard_map/all_to_all | solution.py:238
  56.5 294.7 %all-gather.6.cloned.1.call-start = ((), (), s32[]{:S(2)}) async-start(), calls=%async_computation.4 | async-start | bytes 1179648 | tf_op jit(solution)/shard_map/all_gather | solution.py:112
  368.8 3.2 copy-start.1
  395.3 4.3 %collective-permute-start.1 = (f32[8,3]{1,0:T(8,128)S(1)}, f32[8,3]{1,0:T(8,128)S(1)}, u32[]{:S(2)}, u32[]{:S(2)}) collective-permute-start(f32[8,3]{1,0:T(8,128)S(1)} %get-tuple-element.374), channel_id=1, source_target_pairs={{4,0},{8,4},{12,8},{16,12},{20,16},{24,20},{28,24},{5,1},{9,5},{13... | collective-permute-start | bytes 296 | tf_op jit(solution)/shard_map/ppermute | solution.py:35
  396.6 3.8 collective-permute-start
Sparse Core Ops, SparseCore 0:
  9.6 289.4 all-gather.3
  329.6 21.5 all-gather.5
where the time goes:
time: 412 us; the launch traced here: 408 us
  waiting for transfers between devices  262 us (64%)
  local copies, waits for them, and re-layouts  46.2 us (11%)
  blocking collectives  29.2 us (7%)
  matrix products  23.4 us (6%)
  between operations  15.5 us (4%)
  starting transfers between devices  15.4 us (4%)
  other arithmetic  15.1 us (4%)
    all_gather x1, waiting for transfers between devices, on_device(): lax.all_gather(query_weight, 'grp', axis=0, tiled=True)  239 us
    dot_general x1, local copies, waits for them, and re-layouts, on_device(): jnp.dot(states, lax.all_gather(query_weight, 'grp', axis=0, tiled=True),...  20.7 us
    all_gather x1, waiting for transfers between devices, on_device(): lax.all_gather(window_local, 'ctx', axis=1, tiled=True)  20.2 us
    all_gather x2, blocking collectives, combined_all(): gathered = jax.tree.map(lambda a: lax.all_gather(a, axis), part)  17.6 us
    unnamed x43, local copies, waits for them, and re-layouts  12.4 us
    all_gather x1, blocking collectives, on_device(): lax.all_gather(decode_queries[0], 'ctx', axis=1, tiled=True)  11.6 us
    dot_general x8, matrix products, on_device(): jnp.einsum('wgd,td->gwt', head_queries, key_head_rows, preferred_element_...  10.8 us
    dot_general x1, matrix products, on_device(): jnp.dot(states, lax.all_gather(query_weight, 'grp', axis=0, tiled=True),...  8.72 us
  transfers between devices with their start and end apart: 7, of which 5 were waited for; matrix products, arithmetic and copies ran while one was open for 14% of the time, Pallas kernels for 0%

commit v1 on v0

v1 whole, which is shorter than its diff:
```python
import math

import jax
import jax.numpy as jnp
from jax import lax
from jax.sharding import PartitionSpec as P

KEY_HEADS = 8
HEAD_DIMENSION = 128
BLOCK_POSITIONS = 128
POOL = 7


def rotary_table(positions, head_size):
    exponent = jnp.arange(0, head_size, 2).astype(jnp.float32) / head_size
    inverse = jnp.power(jnp.float32(500000.0), -exponent)
    wavelength = 2.0 * math.pi / inverse
    smooth = (8192.0 / wavelength - 1.0) / 3.0
    blended = (1.0 - smooth) * inverse / 8.0 + smooth * inverse
    adjusted = jnp.where(
        wavelength > 8192.0, inverse / 8.0, jnp.where(wavelength < 2048.0, inverse, blended)
    )
    angles = positions[:, None] * adjusted[None, :]
    return (jnp.cos(angles), jnp.sin(angles))


def rotate(vectors, cosine_table, sine_table):
    half_size = vectors.shape[-1] // 2
    leading = vectors[..., :half_size]
    trailing = vectors[..., half_size:]
    cosine_part = cosine_table[:, None, :]
    sine_part = sine_table[:, None, :]
    return jnp.concatenate(
        [
            leading * cosine_part - trailing * sine_part,
            trailing * cosine_part + leading * sine_part,
        ],
        axis=-1,
    )


def exchange(parts, axis):
    return lax.all_to_all(parts, axis, split_axis=0, concat_axis=0, tiled=True)


def on_device(
    window_states,
    query_weight,
    cache_keys,
    cache_values,
    kept_blocks,
    retained_block_count,
    decode_queries,
    tail_keys,
    tail_values,
    row_lengths,
):
    ctx_count = lax.axis_size("ctx")
    grp_count = lax.axis_size("grp")
    ctx_index = lax.axis_index("ctx")
    states = window_states[0]
    win_rows = states.shape[0]
    depth, local_cols = query_weight.shape
    local_heads = local_cols // HEAD_DIMENSION
    head_total = local_heads * ctx_count
    group_size = head_total // KEY_HEADS
    key_scale = 1.0 / math.sqrt(HEAD_DIMENSION)
    key_head_of = [c * local_heads // group_size for c in range(ctx_count)]
    sharers = group_size // local_heads

    slices = states.reshape(win_rows, grp_count, depth).transpose(1, 0, 2)
    all_slices = exchange(slices, "grp").reshape(grp_count * win_rows, depth)
    partial = jnp.dot(all_slices, query_weight, preferred_element_type=jnp.float32)
    partials = exchange(partial.reshape(grp_count, win_rows, local_cols), "grp")
    projected = jnp.sum(partials, axis=0)

    ctx_local = cache_keys.shape[1]
    total_ctx = ctx_local * ctx_count

    def by_head(rows):
        cells = rows.reshape(rows.shape[0], KEY_HEADS, HEAD_DIMENSION).transpose(1, 0, 2)
        if sharers == 1:
            return cells
        return jnp.repeat(cells, sharers, axis=0)

    keys_out = by_head(cache_keys[0])
    head_keys = exchange(keys_out, "ctx").reshape(total_ctx, HEAD_DIMENSION)

    block_total = ctx_local // BLOCK_POSITIONS
    slots = kept_blocks.shape[2]
    local_blocks = kept_blocks[0] - ctx_index * block_total
    local_counts = retained_block_count[0, :, 0]
    head_range = jnp.arange(KEY_HEADS)

    def kept_rows(rows):
        cells = rows.reshape(block_total, BLOCK_POSITIONS, KEY_HEADS, HEAD_DIMENSION)
        picked = cells[local_blocks, :, head_range[:, None], :]
        picked = picked.reshape(KEY_HEADS, slots * BLOCK_POSITIONS, HEAD_DIMENSION)
        return jnp.repeat(picked, sharers, axis=0) if sharers > 1 else picked

    steps = decode_queries.shape[1]
    rows_local = decode_queries.shape[2]
    tail_len = tail_keys.shape[2]
    own_queries = (
        decode_queries[0]
        .reshape(steps, rows_local, ctx_count, local_heads, HEAD_DIMENSION)
        .transpose(2, 1, 0, 3, 4)
        .reshape(ctx_count, rows_local * steps * local_heads, HEAD_DIMENSION)
    )
    tails = [by_head(t[0].reshape(rows_local * tail_len, -1)) for t in (tail_keys, tail_values)]
    counts_out = jnp.repeat(local_counts, sharers)[:, None]
    lengths_out = jnp.broadcast_to(row_lengths[0][None, :], (ctx_count, rows_local))
    notes = jnp.concatenate([counts_out, lengths_out], axis=1).astype(jnp.bfloat16)
    notes = jnp.pad(notes, ((0, 0), (0, HEAD_DIMENSION - notes.shape[1])))[:, None, :]
    notes = jnp.pad(notes, ((0, 0), (0, 15), (0, 0)))
    pieces = [kept_rows(cache_keys[0]), kept_rows(cache_values[0]), own_queries] + tails + [notes]
    sizes = [p.shape[1] for p in pieces]
    arrived = exchange(jnp.concatenate(pieces, axis=1), "ctx")
    starts = [sum(sizes[:i]) for i in range(len(sizes))]
    got = [arrived[:, s : s + n] for s, n in zip(starts, sizes)]
    kept_keys = got[0].reshape(-1, HEAD_DIMENSION)
    kept_values = got[1].reshape(-1, HEAD_DIMENSION)
    rows_all = ctx_count * rows_local
    queries = got[2].reshape(rows_all, steps * local_heads, HEAD_DIMENSION)
    row_keys = got[3].reshape(rows_all, tail_len, HEAD_DIMENSION)
    row_values = got[4].reshape(rows_all, tail_len, HEAD_DIMENSION)
    all_counts = got[5][:, 0, 0].astype(jnp.int32)
    all_lengths = got[5][:, 0, 1 : 1 + rows_local].astype(jnp.int32).reshape(rows_all)

    live = (jnp.arange(slots)[None, :] < all_counts[:, None]).reshape(-1)
    live = jnp.repeat(live, BLOCK_POSITIONS)[None, None, :]
    cache_scores = (
        jnp.einsum("rqd,td->rqt", queries, kept_keys, preferred_element_type=jnp.float32)
        * key_scale
    )
    cache_scores = jnp.where(live, cache_scores, -1e30)
    step_of = jnp.arange(steps * local_heads) // local_heads
    visible = (
        jnp.arange(tail_len)[None, None, :] < all_lengths[:, None, None] + step_of[None, :, None]
    )
    tail_scores = (
        jnp.einsum("rqd,rjd->rqj", queries, row_keys, preferred_element_type=jnp.float32)
        * key_scale
    )
    tail_scores = jnp.where(visible, tail_scores, -1e30)
    peak = jnp.maximum(
        jnp.max(cache_scores, axis=-1, keepdims=True), jnp.max(tail_scores, axis=-1, keepdims=True)
    )
    cache_weights = jnp.where(live, jnp.exp(cache_scores - peak), 0.0)
    tail_weights = jnp.where(visible, jnp.exp(tail_scores - peak), 0.0)
    numerator = jnp.einsum(
        "rqt,td->rqd",
        cache_weights,
        kept_values.astype(jnp.float32),
        precision=lax.Precision.HIGHEST,
    ) + jnp.einsum(
        "rqj,rjd->rqd",
        tail_weights,
        row_values.astype(jnp.float32),
        precision=lax.Precision.HIGHEST,
    )
    denominator = jnp.sum(cache_weights, axis=-1) + jnp.sum(tail_weights, axis=-1)
    decoded = (numerator / denominator[..., None]).astype(jnp.bfloat16)
    decoded = exchange(
        decoded.reshape(ctx_count, rows_local * steps, local_heads * HEAD_DIMENSION), "ctx"
    )
    decode_out = (
        decoded.reshape(ctx_count, rows_local, steps, local_heads * HEAD_DIMENSION)
        .transpose(2, 1, 0, 3)
        .reshape(1, steps, rows_local, head_total * HEAD_DIMENSION)
    )

    start_pos = total_ctx - win_rows
    positions = (jnp.arange(win_rows) + start_pos).astype(jnp.float32)
    cosine_table, sine_table = rotary_table(positions, HEAD_DIMENSION)
    turned = rotate(
        projected.reshape(win_rows, local_heads, HEAD_DIMENSION), cosine_table, sine_table
    ).astype(jnp.bfloat16)
    allowed = jnp.arange(total_ctx)[None, :] <= (start_pos + jnp.arange(win_rows))[:, None]
    scores = (
        jnp.einsum("wgd,td->gwt", turned, head_keys, preferred_element_type=jnp.float32)
        * key_scale
    )
    scores = jnp.where(allowed[None], scores, -1e30)
    row_max = jnp.max(scores, axis=-1, keepdims=True)
    weights = jnp.where(allowed[None], jnp.exp(scores - row_max), 0.0)
    row_sum = jnp.sum(weights, axis=-1, keepdims=True)
    votes = jnp.sum(weights / row_sum, axis=(0, 1)) * (total_ctx / (win_rows * group_size))
    half_width = (POOL - 1) // 2
    padded = jnp.pad(votes, (half_width, half_width))
    pooled = padded[0:total_ctx]
    for shift_index in range(1, POOL):
        pooled = pooled + padded[shift_index : shift_index + total_ctx]
    shares = exchange((pooled / POOL).reshape(ctx_count, 1, ctx_local), "ctx")
    pooled_votes = jnp.sum(shares.reshape(KEY_HEADS, sharers, ctx_local), axis=1)[None]
    return (pooled_votes, decode_out)


def solution(mesh):
    placed = (
        P("grp", None, None),
        P("grp", "ctx"),
        P("grp", "ctx", None),
        P("grp", "ctx", None),
        P("grp", None, "ctx"),
        P("grp", None, "ctx"),
        P("grp", None, "ctx", None),
        P("grp", "ctx", None, None),
        P("grp", "ctx", None, None),
        P("grp", "ctx"),
    )
    return jax.shard_map(
        on_device,
        mesh=mesh,
        in_specs=placed,
        out_specs=(P("grp", None, "ctx"), P("grp", None, "ctx", None)),
        check_vma=False,
    )
```

time: 412 us -> 122 us (0.30)
  waiting for transfers between devices: 262 us -> 59.5 us
  local copies, waits for them, and re-layouts: 46.2 us -> 15.2 us
  blocking collectives: 29.2 us -> 0 us
  between operations: 15.5 us -> 1.58 us
  starting transfers between devices: 15.4 us -> 25.8 us
  other arithmetic: 15.1 us -> 4.83 us
  matrix products: 23.4 us -> 14.1 us
    all_gather x2 -> x0, waiting for transfers between devices: 259 us -> none  [the longest x1 239 us: on_device(): lax.all_gather(query_weight, 'grp', axis=0, tiled=True)]
    all_to_all x3 -> x6, waiting for transfers between devices: 1.35 us -> 59.5 us  [exchange(): return lax.all_to_all(parts, axis, split_axis=0, concat_axis=0, tiled=True)]
    all_gather x3 -> x0, blocking collectives: 29.2 us -> none  [the longest x2 17.6 us: combined_all(): gathered = jax.tree.map(lambda a: lax.all_gather(a, axis), part)]
    dot_general x1 -> x0, local copies, waits for them, and re-layouts: 20.7 us -> none  [on_device(): jnp.dot(states, lax.all_gather(query_weight, 'grp', axis=0, tiled=True),...]
    dot_general x13 -> x5, matrix products: 23.4 us -> 8.03 us  [the longest x1 4.8 us: on_device(): jnp.dot(all_slices, query_weight, preferred_element_type=jnp.float32)]
    all_to_all x3 -> x6, starting transfers between devices: 10.8 us -> 25.8 us  [exchange(): return lax.all_to_all(parts, axis, split_axis=0, concat_axis=0, tiled=True)]
    reduce_sum x6 -> x3, other arithmetic: 7.99 us -> 1.5 us  [the longest x1 1.11 us: on_device(): jnp.sum(tail_weights, axis=-1)]
    div x0 -> x1, matrix products: none -> 6.02 us  [on_device(): weights / row_sum]
  transfers between devices with their start and end apart: 7 -> 6, of which waited for: 5 -> 5; matrix products, arithmetic and copies ran while one was open for 14% -> 24% of each run, Pallas kernels for 0% -> 0%
where the time goes in v1:
time: 122 us; the launch traced here: 121 us
  waiting for transfers between devices  59.5 us (49%)
  starting transfers between devices  25.8 us (21%)
  local copies, waits for them, and re-layouts  15.2 us (12%)
  matrix products  14.1 us (12%)
  other arithmetic  4.83 us (4%)
  between operations  1.58 us (1%)
    all_to_all x6, waiting for transfers between devices, exchange(): return lax.all_to_all(parts, axis, split_axis=0, concat_axis=0, tiled=True)  59.5 us
    all_to_all x6, starting transfers between devices, exchange(): return lax.all_to_all(parts, axis, split_axis=0, concat_axis=0, tiled=True)  25.8 us
    unnamed x22, local copies, waits for them, and re-layouts  7.21 us
    div x1, matrix products, on_device(): weights / row_sum  6.02 us
    dot_general x1, matrix products, on_device(): jnp.dot(all_slices, query_weight, preferred_element_type=jnp.float32)  4.8 us
    another operation x2, local copies, waits for them, and re-layouts, on_device(): slices = states.reshape(win_rows, grp_count, depth).transpose(1, 0, 2)  3.55 us
  transfers between devices with their start and end apart: 6, of which 5 were waited for; matrix products, arithmetic and copies ran while one was open for 24% of the time, Pallas kernels for 0%

profile of v1, /device:TPU:0, one launch (start us, length us, event | category | flops | bytes accessed | tf_op | source)
XLA Modules:
  0.0 121.0 jit_solution(8256538737604998184)
XLA Ops:
  0.6 1.9 %reshape_squeeze.15 = bf16[64,4,2048]{2,1,0:T(4,128)(2,1)S(1)} reshape(bf16[1,64,8192]{2,1,0:T(8,128)(2,1)} %param.10) | data formatting | bytes 2097152 | tf_op jit(solution)/shard_map/reshape;squeeze | solution.py:71
  2.6 1.6 %copy.78 = bf16[64,4,2048]{2,0,1:T(8,128)(2,1)} copy(bf16[64,4,2048]{2,1,0:T(4,128)(2,1)S(1)} %reshape_squeeze.15) | data formatting | bytes 2097152 | tf_op jit(solution)/shard_map/reshape;squeeze | solution.py:71
  4.2 6.3 %all-to-all-start = ((bf16[4,64,2048]{2,1,0:T(8,128)(2,1)}), bf16[4,64,2048]{2,1,0:T(8,128)(2,1)}, u32[]{:S(2)}, u32[]{:S(2)}) async-start(bf16[4,64,2048]{2,1,0:T(8,128)(2,1)} %bitcast.94), calls=%async_computation | async-start | bytes 2097152 | tf_op jit(solution)/shard_map/all_to_all | solution.py:43
  13.1 0.9 copy.69
  14.8 0.8 constant_dynamic-update-slice_fusion.1
  15.6 0.8 constant_dynamic-update-slice_fusion
  16.4 1.5 %bitcast_dynamic-update-slice_fusion.2 = bf16[8,432,128]{2,1,0:T(8,128)(2,1)} fusion(bf16[8,432,128]{2,1,0:T(8,128)(2,1)} %constant_dynamic-update-slice_fusion, bf16[1,4,64,128]{3,1,2,0:T(4,128)(2,1)} %bitcast.109), kind=kLoop, calls=%fused_computation.45 | loop fusion | bytes 131072
  17.9 0.7 bitcast_dynamic-update-slice_fusion.1
  18.6 0.7 bitcast_dynamic-update-slice_fusion
  19.2 0.6 pad_dynamic-update-slice_fusion
  19.9 16.5 %all-to-all-done = bf16[4,64,2048]{2,1,0:T(8,128)(2,1)} async-done(((bf16[4,64,2048]{2,1,0:T(8,128)(2,1)}), bf16[4,64,2048]{2,1,0:T(8,128)(2,1)}, u32[]{:S(2)}, u32[]{:S(2)}) %all-to-all-start) | async-done | bytes 1048608 | tf_op jit(solution)/shard_map/all_to_all | solution.py:43
  36.4 3.7 %all-to-all-start.4 = ((bf16[8,432,128]{2,1,0:T(8,128)(2,1)}), bf16[8,432,128]{2,1,0:T(8,128)(2,1)S(1)}, u32[]{:S(2)}, u32[]{:S(2)}) async-start(bf16[8,432,128]{2,1,0:T(8,128)(2,1)} %pad_dynamic-update-slice_fusion), calls=%async_computation.4 | async-start | bytes 1769472 | tf_op jit(solution)/shard_map/all_to_all | solution.py:43
  40.4 4.8 %fusion.7 = f32[4,64,1024]{2,1,0:T(8,128)} fusion(bf16[4,64,2048]{2,1,0:T(8,128)(2,1)} %all-to-all-done, bf16[2048,1024]{1,0:T(8,128)(2,1)} %param.11), kind=kOutput, calls=%fused_computation.11 | convolution fusion | flops 1073741824 | bytes 6291456 | tf_op jit(solution)/shard_map/dot_general | solution.py:73
  45.2 8.6 %all-to-all-done.4 = bf16[8,432,128]{2,1,0:T(8,128)(2,1)S(1)} async-done(((bf16[8,432,128]{2,1,0:T(8,128)(2,1)}), bf16[8,432,128]{2,1,0:T(8,128)(2,1)S(1)}, u32[]{:S(2)}, u32[]{:S(2)}) %all-to-all-start.4) | async-done | bytes 884768 | tf_op jit(solution)/shard_map/all_to_all | solution.py:43
  53.7 3.5 %all-to-all-start.1 = ((f32[4,64,1024]{2,1,0:T(8,128)}), f32[4,64,1024]{2,1,0:T(8,128)S(1)}, u32[]{:S(2)}, u32[]{:S(2)}) async-start(f32[4,64,1024]{2,1,0:T(8,128)} %fusion.7), calls=%async_computation.1 | async-start | bytes 2097152 | tf_op jit(solution)/shard_map/all_to_all | solution.py:43
  57.3 0.8 multiply_cosine_fusion
  58.1 1.2 copy.77
  59.9 0.8 fusion.53
  61.2 19.3 %all-to-all-done.1 = f32[4,64,1024]{2,1,0:T(8,128)S(1)} async-done(((f32[4,64,1024]{2,1,0:T(8,128)}), f32[4,64,1024]{2,1,0:T(8,128)S(1)}, u32[]{:S(2)}, u32[]{:S(2)}) %all-to-all-start.1) | async-done | bytes 1048608 | tf_op jit(solution)/shard_map/all_to_all | solution.py:43
  80.5 4.8 %all-to-all-start.2 = ((bf16[8,512,128]{2,1,0:T(8,128)(2,1)}), bf16[8,512,128]{2,1,0:T(8,128)(2,1)}, u32[]{:S(2)}, u32[]{:S(2)}) async-start(bf16[8,512,128]{2,1,0:T(8,128)(2,1)} %bitcast.93), calls=%async_computation.2 | async-start | bytes 2097152 | tf_op jit(solution)/shard_map/all_to_all | solution.py:43
  85.3 1.1 fusion.25
  86.7 0.8 fusion.19
  87.5 1.2 %fusion.15 = bf16[8,32,128]{2,1,0:T(8,128)(2,1)S(1)} fusion(f32[8,32,128]{2,1,0:T(8,128)S(1)} %fusion.19, bf16[8,432,128]{2,1,0:T(8,128)(2,1)S(1)} %all-to-all-done.4, f32[8,32,64]{2,1,0:T(8,128)} %get-tuple-element.13, f32[8,32]{1,0:T(8,128)S(1)} %add.185, f32[8,32]{1,0:T(8,128)S(1)} %max.8, s32[8,32]{1,0:T(8,128)S(1)} %broadcast_add_fusion), kind=kOutput, calls=%fused_computation.22 | convolution fusion | flops 25313280 | bytes 405504 | tf_op jit(solution)/shard_map/rqj,rjd->rqd/dot_general | solution.py:156
  88.7 0.6 reshape.326
  89.5 0.9 subtract_convert_fusion
  90.4 10.3 %all-to-all-done.2 = bf16[8,512,128]{2,1,0:T(8,128)(2,1)} async-done(((bf16[8,512,128]{2,1,0:T(8,128)(2,1)}), bf16[8,512,128]{2,1,0:T(8,128)(2,1)}, u32[]{:S(2)}, u32[]{:S(2)}) %all-to-all-start.2) | async-done | bytes 1048608 | tf_op jit(solution)/shard_map/all_to_all | solution.py:43
  100.7 3.4 %all-to-all-start.5 = ((bf16[8,4,1024]{2,1,0:T(4,128)(2,1)}), bf16[8,4,1024]{2,1,0:T(4,128)(2,1)S(1)}, u32[]{:S(2)}, u32[]{:S(2)}) async-start(bf16[8,4,1024]{2,1,0:T(4,128)(2,1)} %reshape.326), calls=%async_computation.5 | async-start | bytes 131072 | tf_op jit(solution)/shard_map/all_to_all | solution.py:43
  104.1 6.0 %divide_reduce_fusion = f32[4096]{0:T(1024)S(1)} fusion(pred[64,4096]{1,0:T(8,128)(4,1)S(1)} %iota_compare_fusion, bf16[4096,128,1]{1,0,2:T(8,128)(2,1)} %bitcast.4, bf16[64,8,64]{2,1,0:T(8,128)(2,1)S(1)} %get-tuple-element.7, bf16[64,8,64]{2,1,0:T(8,128)(2,1)S(1)} %get-tuple-element.6), kind=kOutput, calls=%fused_computation.10 | convolution fusion | flops 549721088 | bytes 1458176 | tf_op jit(solution)/shard_map/div | solution.py:188
  110.1 0.7 fusion.40
  110.8 4.1 %all-to-all-start.3 = ((f32[8,1,512]{2,1,0:T(1,128)}), f32[8,1,512]{2,1,0:T(1,128)S(1)}, u32[]{:S(2)}, u32[]{:S(2)}) async-start(f32[8,1,512]{2,1,0:T(1,128)} %bitcast.6), calls=%async_computation.3 | async-start | bytes 32768 | tf_op jit(solution)/shard_map/all_to_all | solution.py:43
  115.0 4.8 %all-to-all-done.3 = f32[8,1,512]{2,1,0:T(1,128)S(1)} async-done(((f32[8,1,512]{2,1,0:T(1,128)}), f32[8,1,512]{2,1,0:T(1,128)S(1)}, u32[]{:S(2)}, u32[]{:S(2)}) %all-to-all-start.3) | async-done | bytes 16416 | tf_op jit(solution)/shard_map/all_to_all | solution.py:43
  120.3 0.6 copy.86
  (46 shorter events, 5.0 us)
Async XLA Ops:
  0.6 9.9 %copy-start.3 = (s32[1,8,1]{1,2,0:T(1,128)S(1)}, s32[1,8,1]{1,2,0:T(1,128)}, u32[]{:S(2)}) copy-start(s32[1,8,1]{1,2,0:T(1,128)} %param.14) | copy-start | bytes 100
  0.6 10.1 %copy-start = (bf16[1,512,1024]{2,1,0:T(8,128)(2,1)S(1)}, bf16[1,512,1024]{2,1,0:T(8,128)(2,1)}, u32[]{:S(2)}) copy-start(bf16[1,512,1024]{2,1,0:T(8,128)(2,1)} %param.12) | copy-start | bytes 3145732
  2.6 8.7 %copy-start.1 = (bf16[1,512,1024]{2,1,0:T(8,128)(2,1)S(1)}, bf16[1,512,1024]{2,1,0:T(8,128)(2,1)}, u32[]{:S(2)}) copy-start(bf16[1,512,1024]{2,1,0:T(8,128)(2,1)} %param.13) | copy-start | bytes 3145732
  4.2 32.2 %all-to-all-start = ((bf16[4,64,2048]{2,1,0:T(8,128)(2,1)}), bf16[4,64,2048]{2,1,0:T(8,128)(2,1)}, u32[]{:S(2)}, u32[]{:S(2)}) async-start(bf16[4,64,2048]{2,1,0:T(8,128)(2,1)} %bitcast.94), calls=%async_computation | async-start | bytes 2097152 | tf_op jit(solution)/shard_map/all_to_all | solution.py:43
  11.1 2.0 %copy-start.2 = (bf16[1,1,64,1024]{3,2,1,0:T(8,128)(2,1)S(1)}, bf16[1,1,64,1024]{3,2,1,0:T(8,128)(2,1)}, u32[]{:S(2)}) copy-start(bf16[1,1,64,1024]{3,2,1,0:T(8,128)(2,1)} %param.17) | copy-start | bytes 393220
  11.1 3.6 %copy-start.4 = (s32[1,8,1]{1,2,0:T(1,128)S(1)}, s32[1,8,1]{1,2,0:T(1,128)}, u32[]{:S(2)}) copy-start(s32[1,8,1]{1,2,0:T(1,128)} %param.15) | copy-start | bytes 100
  36.4 17.3 %all-to-all-start.4 = ((bf16[8,432,128]{2,1,0:T(8,128)(2,1)}), bf16[8,432,128]{2,1,0:T(8,128)(2,1)S(1)}, u32[]{:S(2)}, u32[]{:S(2)}) async-start(bf16[8,432,128]{2,1,0:T(8,128)(2,1)} %pad_dynamic-update-slice_fusion), calls=%async_computation.4 | async-start | bytes 1769472 | tf_op jit(solution)/shard_map/all_to_all | solution.py:43
  53.7 26.7 %all-to-all-start.1 = ((f32[4,64,1024]{2,1,0:T(8,128)}), f32[4,64,1024]{2,1,0:T(8,128)S(1)}, u32[]{:S(2)}, u32[]{:S(2)}) async-start(f32[4,64,1024]{2,1,0:T(8,128)} %fusion.7), calls=%async_computation.1 | async-start | bytes 2097152 | tf_op jit(solution)/shard_map/all_to_all | solution.py:43
  80.5 20.2 %all-to-all-start.2 = ((bf16[8,512,128]{2,1,0:T(8,128)(2,1)}), bf16[8,512,128]{2,1,0:T(8,128)(2,1)}, u32[]{:S(2)}, u32[]{:S(2)}) async-start(bf16[8,512,128]{2,1,0:T(8,128)(2,1)} %bitcast.93), calls=%async_computation.2 | async-start | bytes 2097152 | tf_op jit(solution)/shard_map/all_to_all | solution.py:43
  100.7 10.1 %all-to-all-start.5 = ((bf16[8,4,1024]{2,1,0:T(4,128)(2,1)}), bf16[8,4,1024]{2,1,0:T(4,128)(2,1)S(1)}, u32[]{:S(2)}, u32[]{:S(2)}) async-start(bf16[8,4,1024]{2,1,0:T(4,128)(2,1)} %reshape.326), calls=%async_computation.5 | async-start | bytes 131072 | tf_op jit(solution)/shard_map/all_to_all | solution.py:43
  110.8 8.9 %all-to-all-start.3 = ((f32[8,1,512]{2,1,0:T(1,128)}), f32[8,1,512]{2,1,0:T(1,128)S(1)}, u32[]{:S(2)}, u32[]{:S(2)}) async-start(f32[8,1,512]{2,1,0:T(1,128)} %bitcast.6), calls=%async_computation.3 | async-start | bytes 32768 | tf_op jit(solution)/shard_map/all_to_all | solution.py:43
